TPU v7x, 32 devices: a whole 2x2x4 slice. The times are simulated.
32 devices in a mesh: wide: 16 (over z, y, core), narrow: 2 (over x).
Axes of the slice: x: 2, y: 2, z: 4, core: 2. Of those that a mesh axis runs over, the one named last changes fastest.
Arguments:
- hidden_in: bfloat16 [64, 512, 768], P(('wide', 'narrow')), may hold values from -6 to 6
- segment_ids: int32 [64, 512], P(('wide', 'narrow')), may hold values from 0 to 7, never falling along the last dimension, each value on 1 to 256 neighbouring positions
- cotangent: bfloat16 [64, 512, 768], P(('wide', 'narrow')), may hold values from -6 to 6
- attention_weights: float32 [4, 768, 768], P(None, 'wide'), may hold values from -1 to 1
- attention_momentum: float32 [4, 768, 768], P(None, 'wide'), may hold values from -32768 to 32768
- attention_average: float32 [4, 768, 768], P(None, 'wide'), may hold values from -0.21875 to 0.21875
- dense_weights: float32 [2, 768, 3072], P(None, 'wide'), may hold values from -0.21875 to 0.21875
- dense_momentum: float32 [2, 768, 3072], P(None, 'wide'), may hold values from -32768 to 32768
- dense_average: float32 [2, 768, 3072], P(None, 'wide'), may hold values from -0.21875 to 0.21875
- vector_params: float32 [12, 768], P(None, 'wide'), may hold values from -2 to 2
- vector_momentum: float32 [12, 768], P(None, 'wide'), may hold values from -32768 to 32768
- vector_average: float32 [12, 768], P(None, 'wide'), may hold values from -2 to 2
Outputs:
- block_output: bfloat16 [64, 512, 768], P(('wide', 'narrow'))
- grad_input: bfloat16 [64, 512, 768], P(('wide', 'narrow'))
- attention_momentum_new: float32 [4, 768, 768], P(None, 'wide')
- attention_weights_new: float32 [4, 768, 768], P(None, 'wide')
- attention_average_new: float32 [4, 768, 768], P(None, 'wide')
- dense_momentum_new: float32 [2, 768, 3072], P(None, 'wide')
- dense_weights_new: float32 [2, 768, 3072], P(None, 'wide')
- dense_average_new: float32 [2, 768, 3072], P(None, 'wide')
- vector_momentum_new: float32 [12, 768], P(None, 'wide')
- vector_params_new: float32 [12, 768], P(None, 'wide')
- vector_average_new: float32 [12, 768], P(None, 'wide')
Inputs may be any that keep to these rules, and one draw needn't show every extreme that they name: `segment_ids`: ids never fall along a row; tokens with equal ids in a row form one document or the padding.
All inputs are finite; a program needn't handle non-finite values.
Results may differ from a plain program's by a relative error of at most 0.015.
The roundings to bfloat16 on the way count: a program that leaves them out, or rounds other values in their place, can miss the bound.
Values may be sent and summed in bfloat16 or wider, within the bound.
A program may use at most 192 MiB of HBM per device.

v0:
```python
import functools, math
import jax, jax.numpy as jnp
from jax import lax
from jax.sharding import PartitionSpec as P
from jax.experimental import pallas as pl
from jax.experimental.pallas import tpu as pltpu

HD = 64
LOG2E = 1.4426950408889634
SCALE2 = 0.125 * LOG2E
NEG = -1e30
EPS = 1e-12
momentum_decay = 0.5
average_decay = 0.5
matrix_rate = 0.03
vector_rate = 0.3
f32, bf16 = jnp.float32, jnp.bfloat16
BIG = 60 * 2**20

def dot(a, b):
    return lax.dot_general(a, b, (((1,), (0,)), ((), ())), preferred_element_type=f32)
def dot_nt(a, b):
    return lax.dot_general(a, b, (((1,), (1,)), ((), ())), preferred_element_type=f32)
def dot_tn(a, b):
    return lax.dot_general(a, b, (((0,), (0,)), ((), ())), preferred_element_type=f32)

def key_range(c, seq, blk):
    lo = max(0, c * blk - seq // 2 + 1) // blk * blk
    hi = min(seq, -(-((c + 1) * blk - 1 + seq // 2) // blk) * blk)
    return lo, hi

def fill_bias(seg_ref, bias_ref):
    segf = seg_ref[0].astype(f32)
    seq = segf.shape[1]
    rep = jnp.broadcast_to(segf, (128, seq)).T
    for j in range(seq // 128):
        bias_ref[:, j * 128:(j + 1) * 128] = jnp.where(rep == segf[:, j * 128:(j + 1) * 128], 0.0, NEG)

def fwd_kernel(blk, x_ref, seg_ref, w_ref, b_ref, qkv_ref, c_ref, lse_ref, bias_ref, lsea_ref):
    seq, width = x_ref.shape
    x = x_ref[...]
    for j in range(3):
        sl = slice(j * width, (j + 1) * width)
        qkv_ref[:, sl] = (dot(x, w_ref[:, sl]) + b_ref[:, sl]).astype(bf16)
    fill_bias(seg_ref, bias_ref)
    lane = lax.broadcasted_iota(jnp.int32, (blk, 128), 1)
    first = lane < HD
    ones = jnp.ones((seq, 128), bf16)
    def pair(p, _):
        col = pl.multiple_of(p * 128, 128)
        q2 = qkv_ref[:, pl.ds(col, 128)]
        k2 = qkv_ref[:, pl.ds(col + width, 128)]
        v2 = jnp.concatenate([qkv_ref[:, pl.ds(col + 2 * width, 128)], ones], 1)
        for c in range(seq // blk):
            lo, hi = key_range(c, seq, blk)
            rows = slice(c * blk, (c + 1) * blk)
            qc = q2[rows]
            outs = []
            la = lsea_ref[rows, :]
            for h in range(2):
                qm = jnp.where(first if h == 0 else ~first, qc, jnp.zeros_like(qc))
                s = dot_nt(qm, k2[lo:hi]) + bias_ref[rows, lo:hi]
                m = jnp.max(s, 1, keepdims=True)
                e = jnp.exp2((s - m) * SCALE2)
                o = dot(e.astype(bf16), v2[lo:hi])
                l = o[:, 128:]
                outs.append(o[:, :128] / l)
                la = jnp.where(lane == 2 * p + h, m * SCALE2 + jnp.log(l) * LOG2E, la)
            lsea_ref[rows, :] = la
            c_ref[rows, pl.ds(col, 128)] = jnp.where(first, outs[0], outs[1]).astype(bf16)
        return 0
    lax.fori_loop(0, width // 128, pair, 0)
    lse_ref[0] = lsea_ref[...].T[:lse_ref.shape[1]]

def attn_fwd(x, seg, w, b, blk=128):
    rows, seq = seg.shape
    width = x.shape[1]
    return pl.pallas_call(
        functools.partial(fwd_kernel, blk), grid=(rows,),
        out_shape=(jax.ShapeDtypeStruct((rows * seq, 3 * width), bf16), jax.ShapeDtypeStruct((rows * seq, width), bf16),
                   jax.ShapeDtypeStruct((rows, 16, seq), f32)),
        in_specs=[pl.BlockSpec((seq, width), lambda r: (r, 0)), pl.BlockSpec((1, 1, seq), lambda r: (r, 0, 0)),
                  pl.BlockSpec((width, 3 * width), lambda r: (0, 0)), pl.BlockSpec((1, 3 * width), lambda r: (0, 0))],
        out_specs=(pl.BlockSpec((seq, 3 * width), lambda r: (r, 0)), pl.BlockSpec((seq, width), lambda r: (r, 0)),
                   pl.BlockSpec((1, 16, seq), lambda r: (r, 0, 0))),
        scratch_shapes=[pltpu.VMEM((seq, seq), f32), pltpu.VMEM((seq, 128), f32)],
        compiler_params=pltpu.CompilerParams(vmem_limit_bytes=BIG),
        name="attn_fwd",
    )(x, seg.reshape(rows, 1, seq), w, b)

def bwd_kernel(blk, seg_ref, qkv_ref, dc_ref, lse_ref, delta_ref, dh1_ref, w_ref, x_ref, dqkv_ref, gin_ref, dw_ref, db_ref, bias_ref, ds_ref, acc_ref):
    r = pl.program_id(0)
    seq = dc_ref.shape[0]
    width = dc_ref.shape[1]
    fill_bias(seg_ref, bias_ref)
    ds_ref[...] = jnp.zeros_like(ds_ref)
    lane = lax.broadcasted_iota(jnp.int32, (blk, 128), 1)
    first = lane < HD
    lane_s = lax.broadcasted_iota(jnp.int32, (seq, 128), 1)
    def pair(p, _):
        col = pl.multiple_of(p * 128, 128)
        q2 = qkv_ref[:, pl.ds(col, 128)]
        k2 = qkv_ref[:, pl.ds(col + width, 128)]
        v2 = qkv_ref[:, pl.ds(col + 2 * width, 128)]
        dc2 = dc_ref[:, pl.ds(col, 128)]
        dqs = []
        for h in range(2):
            lse = lse_ref[0, pl.ds(2 * p + h, 1), :]
            dl = delta_ref[pl.ds(2 * p + h, 1), :]
            mine = first if h == 0 else ~first
            for c in range(seq // blk):
                lo, hi = key_range(c, seq, blk)
                rows = slice(c * blk, (c + 1) * blk)
                kc, vc = k2[rows], v2[rows]
                km = jnp.where(mine, kc, jnp.zeros_like(kc))
                vm = jnp.where(mine, vc, jnp.zeros_like(vc))
                st = dot_nt(km, q2[lo:hi])
                pt = jnp.exp2((st + bias_ref[rows, lo:hi]) * SCALE2 - lse[:, lo:hi])
                dp = dot_nt(vm, dc2[lo:hi])
                ds = (pt * (dp - dl[:, lo:hi])).astype(bf16)
                ds_ref[h, rows, lo:hi] = ds
                dv = dot(pt.astype(bf16), dc2[lo:hi])
                dk = dot(ds, q2[lo:hi]) * 0.125
                if h == 0:
                    dqkv_ref[rows, pl.ds(col + 2 * width, 128)] = dv.astype(bf16)
                    dqkv_ref[rows, pl.ds(col + width, 128)] = dk.astype(bf16)
                else:
                    ov = dqkv_ref[rows, pl.ds(col + 2 * width, 128)]
                    ok = dqkv_ref[rows, pl.ds(col + width, 128)]
                    dqkv_ref[rows, pl.ds(col + 2 * width, 128)] = jnp.where(first, ov, dv.astype(bf16))
                    dqkv_ref[rows, pl.ds(col + width, 128)] = jnp.where(first, ok, dk.astype(bf16))
            dqs.append(dot_tn(ds_ref[h], k2) * 0.125)
        dqkv_ref[:, pl.ds(col, 128)] = jnp.where(lane_s < HD, dqs[0], dqs[1]).astype(bf16)
        return 0
    lax.fori_loop(0, width // 128, pair, 0)
    dqkv = dqkv_ref[...]
    gin_ref[...] = (dh1_ref[...] + dot_nt(dqkv, w_ref[...])).astype(bf16)
    x = x_ref[...]
    for j in range(3):
        sl = slice(j * width, (j + 1) * width)
        d = dot_tn(x, dqkv[:, sl])
        s = jnp.sum(dqkv[:, sl].astype(f32), 0, keepdims=True)
        @pl.when(r == 0)
        def _():
            acc_ref[:, sl] = d
            db_ref[:, sl] = s
        @pl.when(r == pl.num_programs(0) - 1)
        def _():
            dw_ref[:, sl] = (acc_ref[:, sl] + d).astype(bf16)
            db_ref[:, sl] += s

def attn_bwd(seg, qkv, dc, lse, delta, dh1, w, x, blk=128):
    rows, seq = seg.shape
    width = dc.shape[1]
    assert rows == 2
    return pl.pallas_call(
        functools.partial(bwd_kernel, blk), grid=(rows,),
        out_shape=(jax.ShapeDtypeStruct((rows * seq, 3 * width), bf16), jax.ShapeDtypeStruct((rows * seq, width), bf16),
                   jax.ShapeDtypeStruct((width, 3 * width), bf16), jax.ShapeDtypeStruct((1, 3 * width), f32)),
        in_specs=[pl.BlockSpec((1, 1, seq), lambda r: (r, 0, 0)), pl.BlockSpec((seq, 3 * width), lambda r: (r, 0)),
                  pl.BlockSpec((seq, width), lambda r: (r, 0)), pl.BlockSpec((1, 16, seq), lambda r: (r, 0, 0)),
                  pl.BlockSpec((16, seq), lambda r: (0, r)), pl.BlockSpec((seq, width), lambda r: (r, 0)),
                  pl.BlockSpec((width, 3 * width), lambda r: (0, 0)), pl.BlockSpec((seq, width), lambda r: (r, 0))],
        out_specs=(pl.BlockSpec((seq, 3 * width), lambda r: (r, 0)), pl.BlockSpec((seq, width), lambda r: (r, 0)),
                   pl.BlockSpec((width, 3 * width), lambda r: (0, 0)), pl.BlockSpec((1, 3 * width), lambda r: (0, 0))),
        scratch_shapes=[pltpu.VMEM((seq, seq), f32), pltpu.VMEM((2, seq, seq), bf16), pltpu.VMEM((width, 3 * width), f32)],
        compiler_params=pltpu.CompilerParams(vmem_limit_bytes=BIG),
        name="attn_bwd",
    )(seg.reshape(rows, 1, seq), qkv, dc, lse, delta, dh1, w, x)

RSQRT_2PI = 1.0 / math.sqrt(2 * math.pi)
def gelu_parts(u):
    phi_cdf = 0.5 + 0.5 * lax.erf(u * math.sqrt(0.5))
    dens = jnp.exp2(u * u * (-0.5 * LOG2E)) * RSQRT_2PI
    return u * phi_cdf, phi_cdf + u * dens

def mid_kernel(chunk, x_ref, c_ref, e_ref, wo_ref, win_ref, wd_ref, v_ref, bin_ref,
               out_ref, y1_ref, g_ref, dz_ref, du_ref, da_ref, dc_ref, dh1_ref, delta_ref, dv_ref, dbin_ref, gp_ref):
    i = pl.program_id(0)
    blk, width = x_ref.shape
    ff = win_ref.shape[1]
    @pl.when(i == 0)
    def _():
        dv_ref[...] = jnp.zeros_like(dv_ref)
        dbin_ref[...] = jnp.zeros_like(dbin_ref)
    g1, s1, g2, s2, bo, bd = (v_ref[j:j + 1, :] for j in (0, 1, 2, 3, 6, 7))
    cb = c_ref[...]
    h1 = x_ref[...].astype(f32) + (dot(cb, wo_ref[...]) + bo)
    cen = h1 - jnp.mean(h1, 1, keepdims=True)
    r1 = lax.rsqrt(jnp.mean(cen * cen, 1, keepdims=True) + EPS)
    n1 = cen * r1
    y1 = n1 * g1 + s1
    y1l = y1.astype(bf16)
    y1_ref[...] = y1l
    z = jnp.zeros((blk, width), f32)
    for j in range(ff // chunk):
        sl = slice(j * chunk, (j + 1) * chunk)
        u = dot(y1l, win_ref[:, sl]) + bin_ref[:, sl]
        g, gp = gelu_parts(u)
        gl = g.astype(bf16)
        g_ref[:, sl] = gl
        gp_ref[:, sl] = gp
        z += dot_nt(gl, wd_ref[:, sl])
    h2 = y1 + (z + bd)
    cen = h2 - jnp.mean(h2, 1, keepdims=True)
    r2 = lax.rsqrt(jnp.mean(cen * cen, 1, keepdims=True) + EPS)
    n2 = cen * r2
    out_ref[...] = (n2 * g2 + s2).astype(bf16)
    e = e_ref[...].astype(f32)
    eg = e * g2
    dh2 = r2 * (eg - jnp.mean(eg, 1, keepdims=True) - n2 * jnp.mean(eg * n2, 1, keepdims=True))
    dz = dh2.astype(bf16)
    dz_ref[...] = dz
    dy1 = dh2
    for j in range(ff // chunk):
        sl = slice(j * chunk, (j + 1) * chunk)
        du = (dot(dz, wd_ref[:, sl]) * gp_ref[:, sl]).astype(bf16)
        du_ref[:, sl] = du
        dbin_ref[:, sl] += jnp.sum(du.astype(f32), 0, keepdims=True)
        dy1 += dot_nt(du, win_ref[:, sl])
    dn = dy1 * g1
    dh1 = r1 * (dn - jnp.mean(dn, 1, keepdims=True) - n1 * jnp.mean(dn * n1, 1, keepdims=True))
    dh1_ref[...] = dh1
    da = dh1.astype(bf16)
    da_ref[...] = da
    dc = dot_nt(da, wo_ref[...]).astype(bf16)
    dc_ref[...] = dc
    prod = dc.astype(f32) * cb.astype(f32)
    hi = prod.astype(bf16)
    lo = (prod - hi.astype(f32)).astype(bf16)
    sel = jnp.where(lax.broadcasted_iota(jnp.int32, (16, width), 0) == lax.broadcasted_iota(jnp.int32, (16, width), 1) // HD, 1.0, 0.0).astype(bf16)
    delta_ref[...] = dot_nt(sel, hi) + dot_nt(sel, lo)
    parts = [dy1 * n1, dy1, e * n2, e, da.astype(f32), dz.astype(f32)]
    for j, t in zip((0, 1, 2, 3, 6, 7), parts):
        dv_ref[j:j + 1, :] += jnp.sum(t, 0, keepdims=True)

def mid(x, c, e, wo, win, wd, vec, bin_, blk=256, chunk=768):
    n, width = x.shape
    ff = win.shape[1]
    tok = lambda w: pl.BlockSpec((blk, w), lambda i: (i, 0))
    full = lambda a: pl.BlockSpec(a.shape, lambda i: (0, 0), pipeline_mode=pl.Buffered(1))
    sh = jax.ShapeDtypeStruct
    return pl.pallas_call(
        functools.partial(mid_kernel, chunk), grid=(n // blk,),
        out_shape=(sh((n, width), bf16), sh((n, width), bf16), sh((n, ff), bf16), sh((n, width), bf16), sh((n, ff), bf16),
                   sh((n, width), bf16), sh((n, width), bf16), sh((n, width), f32), sh((16, n), f32), sh((8, width), f32), sh((1, ff), f32)),
        in_specs=[tok(width), tok(width), tok(width), full(wo), full(win), full(wd), full(vec), full(bin_)],
        out_specs=(tok(width), tok(width), tok(ff), tok(width), tok(ff), tok(width), tok(width), tok(width),
                   pl.BlockSpec((16, blk), lambda i: (0, i)), pl.BlockSpec((8, width), lambda i: (0, 0)), pl.BlockSpec((1, ff), lambda i: (0, 0))),
        scratch_shapes=[pltpu.VMEM((blk, ff), f32)],
        compiler_params=pltpu.CompilerParams(vmem_limit_bytes=BIG),
        name="middle",
    )(x, c, e, wo, win, wd, vec, bin_)

def wgrad_kernel(a_ref, b_ref, o_ref):
    o_ref[...] = dot_tn(a_ref[...], b_ref[...]).astype(bf16)

def wgrad(a, b, blk=768):
    n, m = a.shape
    k = b.shape[1]
    return pl.pallas_call(wgrad_kernel, grid=(k // blk,), out_shape=jax.ShapeDtypeStruct((m, k), bf16),
        in_specs=[pl.BlockSpec((n, m), lambda j: (0, 0)), pl.BlockSpec((n, blk), lambda j: (0, j))],
        out_specs=pl.BlockSpec((m, blk), lambda j: (0, j)),
        compiler_params=pltpu.CompilerParams(vmem_limit_bytes=BIG), name="wgrad")(a, b)


LANES = 128
PIECE = 3 * LANES
GATHER_LAGS = (0, 2, 4, 6)
REDUCE_LAGS = (2, 4, 6, 8)
AHEAD = 3
MESH = pl.DeviceIdType.MESH


class Place:
    def __init__(self):
        self.w = lax.axis_index("wide")
        self.x = lax.axis_index("narrow")
        self.core = lax.rem(self.w, 2)
        self.y = lax.rem(self.w // 2, 2)
        self.b = lax.rem(self.w // 4, 2)
        self.a = self.w // 8
        self.z = self.w // 4

    def z_peer(self, k):
        return lax.rem(self.z + k, 4)

    def over(self, name):
        if name == "x":
            return (self.w, 1 - self.x)
        if name in (1, 2, 3):
            return (4 * self.z_peer(name) + lax.rem(self.w, 4), self.x)
        step = {"a": 8, "b": 4, "y": 2, "core": 1}[name]
        return (self.w + step * (1 - 2 * getattr(self, name)), self.x)

    near = ("a", "b", "y", "x", "core")
    reduce_peers = (1, 2, 3, "y", "x", "core")

    def greet(self, names):
        for name in names:
            pl.semaphore_signal(pltpu.get_barrier_semaphore(), inc=1, device_id=self.over(name), device_id_type=MESH)

    def met(self, names):
        pl.semaphore_wait(pltpu.get_barrier_semaphore(), len(names))


def remote(src, dst, send, recv, device):
    return pltpu.make_async_remote_copy(src_ref=src, dst_ref=dst, send_sem=send, recv_sem=recv, device_id=device, device_id_type=MESH)


def when(condition, step):
    @pl.when(condition)
    def _():
        step()


def loop(count, step):
    lax.fori_loop(0, count, lambda i, _: (step(i), 0)[1], 0)


class Gather:
    def __init__(self, place, shard, full, sems, pieces):
        self.p, self.shard, self.full, self.pieces = place, shard, full, pieces
        self.sems = {name: (sems[2 * k], sems[2 * k + 1]) for k, name in enumerate(("a", "b", "y", "x", "core"))}
        self.kept = sems[10]
        self.own = pl.ds(place.x, 2)

    def mine(self, i, a):
        return self.full.at[i, self.own, a, self.p.b, self.p.y, self.p.core]

    def keep(self, i):
        return pltpu.make_async_copy(self.shard.at[i, self.own], self.mine(i, self.p.a), self.kept.at[i])

    def copy(self, name, i, incoming=False):
        p, f = self.p, self.full
        at = {n: (1 - getattr(p, n) if incoming and n == name else getattr(p, n)) for n in ("a", "b", "y", "x", "core")}
        every = slice(None)
        if name == "a":
            dst = self.mine(i, at["a"])
            src = self.shard.at[i, self.own]
        else:
            if name == "b":
                dst = f.at[i, self.own, :, at["b"], p.y, p.core]
            elif name == "y":
                dst = f.at[i, self.own, :, :, at["y"], p.core]
            elif name == "x":
                dst = f.at[i, 2 * at["x"], :, :, :, p.core]
            else:
                dst = f.at[i, :, :, :, :, at["core"]]
            src = dst
        send, recv = self.sems[name]
        return remote(src, dst, send.at[i], recv.at[i], p.over(name))

    def start(self, i):
        self.keep(i).start()
        self.copy("a", i).start()

    def b_step(self, i):
        self.keep(i).wait()
        self.copy("a", i, True).wait_recv()
        self.copy("b", i).start()

    def y_step(self, i):
        self.copy("b", i, True).wait_recv()
        self.copy("y", i).start()

    def x_step(self, i):
        self.copy("y", i, True).wait_recv()
        self.copy("x", i).start()

    def core_step(self, i):
        self.copy("x", i, True).wait_recv()
        self.copy("core", i).start()

    def arrive(self, i):
        self.copy("core", i, True).wait_recv()

    def turn(self, t):
        for k in range(2):
            ahead = AHEAD + 2 * t + k
            when(ahead < self.pieces, lambda ahead=ahead: self.start(ahead))
        for lag, step in zip(GATHER_LAGS, (self.b_step, self.y_step, self.x_step, self.core_step)):
            when((t >= lag) & (t < self.pieces + lag), lambda lag=lag, step=step: step(t - lag))

    def sent(self, i):
        for name in ("a", "b", "y", "x", "core"):
            self.copy(name, i).wait_send()


class GatherVector:
    def __init__(self, place, shard, full, sems):
        self.p, self.shard, self.full = place, shard, full
        self.sems = {name: (sems[2 * k], sems[2 * k + 1]) for k, name in enumerate(("a", "b", "y", "core"))}
        self.kept = sems[8]

    def keep(self):
        p = self.p
        return pltpu.make_async_copy(self.shard, self.full.at[p.a, p.b, p.y, p.core], self.kept)

    def copy(self, name, incoming=False):
        p = self.p
        at = {n: (1 - getattr(p, n) if incoming and n == name else getattr(p, n)) for n in ("a", "b", "y", "core")}
        every = slice(None)
        first = ("a", "b", "y", "core").index(name)
        dst = self.full.at[tuple(at[n] if n == name or n == "core" or k > first else every for k, n in enumerate(("a", "b", "y", "core")))]
        src = self.shard if name == "a" else dst
        send, recv = self.sems[name]
        return remote(src, dst, send, recv, p.over(name))

    def start(self):
        self.keep().start()
        self.copy("a").start()

    def step(self, name, then):
        if name == "a":
            self.keep().wait()
        self.copy(name, True).wait_recv()
        self.copy(then).start()

    def arrive(self):
        self.copy("core", True).wait_recv()

    def sent(self):
        for name in ("a", "b", "y", "core"):
            self.copy(name).wait_send()


def tile(ref, i, t):
    rows = 16 * ref.shape[-2]
    return ref[i, t].reshape(rows, LANES)


def columns(ref, *pieces):
    return jnp.concatenate([tile(ref, i, t) for i in pieces for t in range(3)], 1)


def doc_bias(seg_row, bias_ref, r):
    segf = seg_row.astype(f32)
    seq = segf.shape[1]
    rep = jnp.broadcast_to(segf, (LANES, seq)).T
    for j in range(seq // LANES):
        sl = slice(j * LANES, (j + 1) * LANES)
        bias_ref[r, :, sl] = jnp.where(rep == segf[:, sl], 0.0, NEG)


def stage_kernel(heads, x_hbm, seg_ref, e_hbm, aw_hbm, dw_hbm, vp_ref,
                 qkv_o, c_o, lse_o, w_o, out_o, y1_o, g_o, gp_o, dz_o, dh2_o, n1_o, r1_o, dv_o, vrow,
                 full, vfull, shard, vshard, square, xb, eb, cb, n1b, y1b, acc, gp, gb, dzb, bias, lsea, binr, r1b,
                 in_sem, out_sem, w_sem, two_sem, *sems):
    place = Place()
    rows, seq = seg_ref.shape
    tokens, width = x_hbm.shape
    pairs = heads // 2
    pieces = shard.shape[0]
    chunks = gb.shape[0]
    own_rows = aw_hbm.shape[1]
    blk = 256
    big = 512
    g = Gather(place, shard, full, sems[:11], pieces)
    gv = GatherVector(place, vshard, vfull, sems[11:])

    loads = [pltpu.make_async_copy(aw_hbm.at[k], gp.at[0, pl.ds(k * own_rows, own_rows)], in_sem.at[k]) for k in range(4)]
    for k in range(2):
        for j in range(chunks):
            loads.append(pltpu.make_async_copy(
                dw_hbm.at[k, :, pl.ds(j * width, width)], gp.at[1 + k, pl.ds(j * own_rows, own_rows)], in_sem.at[4 + k * chunks + j]))
    n = len(loads)
    x_load = pltpu.make_async_copy(x_hbm, xb, in_sem.at[n])
    e_load = pltpu.make_async_copy(e_hbm, eb, in_sem.at[n + 1])
    for c in loads:
        c.start()
    place.greet(place.near)
    x_load.start()
    e_load.start()
    square[...] = jnp.zeros_like(square)
    lsea[...] = jnp.zeros_like(lsea)
    square[: vp_ref.shape[0], :own_rows] = vp_ref[...]
    vshard[...] = square[...].T[:own_rows].astype(bf16)

    def own_tile(k, j, t):
        return gp[k, j * own_rows : (j + 1) * own_rows, t * LANES : (t + 1) * LANES].astype(bf16)

    for c in loads[:3]:
        c.wait()
    for p in range(pairs):
        for t in range(3):
            shard[p, t] = own_tile(0, t, p)
    place.met(place.near)
    gv.start()
    for i in range(AHEAD):
        g.start(i)
    for c in loads[3:]:
        c.wait()
    for t in range(6):
        shard[pairs + t // 3, t % 3] = own_tile(0, 3, t)
        for j in range(chunks):
            for k in range(2):
                shard[pairs + 2 + 4 * j + 2 * k + t // 3, t % 3] = own_tile(1 + k, j, t)
    for r in range(rows):
        doc_bias(seg_ref[r : r + 1, :], bias, r)
    gv.step("a", "b")
    fill = GATHER_LAGS[-1] + 1
    for t in range(fill):
        g.turn(t)
        if t == 1:
            gv.step("b", "y")
        if t == 4:
            gv.step("y", "core")
    gv.arrive()
    vec = vfull[...].reshape(16 * own_rows, LANES).astype(f32).T
    vrow[...] = vec[: vrow.shape[0]]
    for j in range(chunks):
        binr[j] = vrow[8 + j : 9 + j, :]
    x_load.wait()

    first = lax.broadcasted_iota(jnp.int32, (LANES, LANES), 1) < HD
    lane = lax.broadcasted_iota(jnp.int32, (LANES, LANES), 1)
    ones = jnp.ones((seq, LANES), bf16)

    def qkv_at(p):
        return gb.at[p // 2, :, pl.ds(pl.multiple_of(lax.rem(p, 2) * PIECE, LANES), PIECE)]

    def qkv_out(p):
        return pltpu.make_async_copy(qkv_at(p), qkv_o.at[p], out_sem.at[p])

    def w_out(i):
        return pltpu.make_async_copy(full.at[i], w_o.at[i], w_sem.at[i])

    def pair(p):
        g.arrive(p)
        w_out(p).start()
        head = pl.ds(pl.multiple_of(p * LANES, LANES), LANES)
        w = columns(full, p)
        b = jnp.concatenate([vrow[4:5, head], jnp.zeros((1, LANES), f32), vrow[5:6, head]], 1)
        col = pl.multiple_of(lax.rem(p, 2) * PIECE, LANES)
        gb[p // 2, :, pl.ds(col, PIECE)] = (dot(xb[...], w) + b).astype(bf16)
        qkv_out(p).start()

        def row(r):
            tok = pl.ds(pl.multiple_of(r * seq, seq), seq)
            q2 = gb[p // 2, tok, pl.ds(col, LANES)]
            k2 = gb[p // 2, tok, pl.ds(col + LANES, LANES)]
            v2 = jnp.concatenate([gb[p // 2, tok, pl.ds(col + 2 * LANES, LANES)], ones], 1)
            for c in range(seq // LANES):
                lo, hi = key_range(c, seq, LANES)
                cut = slice(c * LANES, (c + 1) * LANES)
                outs = []
                la = lsea[r, cut, :]
                for h in range(2):
                    qm = jnp.where(first if h == 0 else ~first, q2[cut], jnp.zeros_like(q2[cut]))
                    s = dot_nt(qm, k2[lo:hi]) + bias[r, cut, lo:hi]
                    m = jnp.max(s, 1, keepdims=True)
                    o = dot(jnp.exp2((s - m) * SCALE2).astype(bf16), v2[lo:hi])
                    l = o[:, LANES:]
                    outs.append(o[:, :LANES] / l)
                    la = jnp.where(lane == 2 * p + h, m * SCALE2 + jnp.log(l) * LOG2E, la)
                lsea[r, cut, :] = la
                cb[pl.ds(pl.multiple_of(r * seq + c * LANES, LANES), LANES), head] = jnp.where(first, outs[0], outs[1]).astype(bf16)
            g.turn(fill + 2 * p + r)

        loop(rows, row)

    loop(pairs, pair)
    done = fill + 2 * pairs
    for r in range(rows):
        lse_o[r] = lsea[r].T[: lse_o.shape[1]]
    c_out = pltpu.make_async_copy(cb, c_o, out_sem.at[pairs])
    c_out.start()
    g1, s1, g2, s2, bo, bd = (vrow[j : j + 1, :] for j in (0, 1, 2, 3, 6, 7))

    def block(i):
        return pl.ds(pl.multiple_of(i * blk, blk), blk)

    for i in (pairs, pairs + 1):
        g.arrive(i)
        w_out(i).start()

    def norm_one(i):
        at = block(i)
        h1 = xb[at, :].astype(f32) + (dot(cb[at, :], columns(full, pairs, pairs + 1)) + bo)
        cen = h1 - jnp.mean(h1, 1, keepdims=True)
        r1 = lax.rsqrt(jnp.mean(cen * cen, 1, keepdims=True) + EPS)
        n1 = cen * r1
        y1 = n1 * g1 + s1
        n1b[at, :] = n1
        r1b[at, :] = jnp.broadcast_to(r1, (blk, LANES))
        y1b[at, :] = y1.astype(bf16)
        acc[at, :] = y1 + bd
        when(lax.rem(i, 2) == 1, lambda: g.turn(done + i // 2))

    loop(tokens // blk, norm_one)
    done += 2
    y1_out = pltpu.make_async_copy(y1b, y1_o, out_sem.at[pairs + 2])
    y1_out.start()
    n1_out = pltpu.make_async_copy(n1b, n1_o, out_sem.at[pairs + 1])
    n1_out.start()
    r1_out = pltpu.make_async_copy(r1b, r1_o, out_sem.at[pairs + 5 + chunks])
    r1_out.start()
    loop(pairs, lambda p: qkv_out(p).wait())

    def up(j):
        return columns(full, pairs + 2 + 4 * j, pairs + 3 + 4 * j)

    def down(j):
        return columns(full, pairs + 4 + 4 * j, pairs + 5 + 4 * j)

    def g_out(j):
        return pltpu.make_async_copy(gb.at[j], g_o.at[j], out_sem.at[pairs + 7 + j])

    def gp_out(j):
        return pltpu.make_async_copy(gp.at[j], gp_o.at[j], out_sem.at[pairs + 7 + chunks + j])

    def ff_chunk(j):
        def ready(k):
            for t in (k, k + 1):
                g.arrive(pairs + 2 + 4 * j + t)
                w_out(pairs + 2 + 4 * j + t).start()

        def up_block(i):
            at = pl.ds(pl.multiple_of(i * big, big), big)
            act, slope = gelu_parts(dot(y1b[at, :], up(j)) + binr[j])
            gb[j, at, :] = act.astype(bf16)
            gp[j, at, :] = slope
            g.turn(done + 4 * j + i)

        def down_block(i):
            at = pl.ds(pl.multiple_of(i * big, big), big)
            acc[at, :] += dot_nt(gb[j, at, :], down(j))
            g.turn(done + 4 * j + 2 + i)

        ready(0)
        loop(tokens // big, up_block)
        g_out(j).start()
        gp_out(j).start()
        ready(2)
        loop(tokens // big, down_block)

    loop(chunks, ff_chunk)
    e_load.wait()
    dv_o[...] = jnp.zeros_like(dv_o)

    def colsum(t):
        return jnp.sum(t, 0, keepdims=True)

    def norm_two(i):
        at = block(i)
        h2 = acc[at, :]
        cen = h2 - jnp.mean(h2, 1, keepdims=True)
        r2 = lax.rsqrt(jnp.mean(cen * cen, 1, keepdims=True) + EPS)
        n2 = cen * r2
        xb[at, :] = (n2 * g2 + s2).astype(bf16)
        e = eb[at, :].astype(f32)
        eg = e * g2
        dh2 = r2 * (eg - jnp.mean(eg, 1, keepdims=True) - n2 * jnp.mean(eg * n2, 1, keepdims=True))
        dz = dh2.astype(bf16)
        dzb[at, :] = dz
        acc[at, :] = dh2
        dv_o[2:3, :] += colsum(e * n2)
        dv_o[3:4, :] += colsum(e)
        dv_o[7:8, :] += colsum(dz.astype(f32))

    def norm_two_out(i):
        at = block(i)
        pairs_of = ((xb, out_o), (dzb, dz_o), (acc, dh2_o))
        return [pltpu.make_async_copy(src.at[at], dst.at[at], two_sem.at[k, i]) for k, (src, dst) in enumerate(pairs_of)]

    def norm_two_step(i):
        norm_two(i)
        for c in norm_two_out(i):
            c.start()

    loop(tokens // blk, norm_two_step)
    gv.sent()
    loop(pieces, g.sent)
    loop(pieces, lambda i: w_out(i).wait())
    for c in [c_out, y1_out, n1_out, r1_out]:
        c.wait()
    for i in range(tokens // blk):
        for c in norm_two_out(i):
            c.wait()
    loop(chunks, lambda j: g_out(j).wait())
    loop(chunks, lambda j: gp_out(j).wait())


def stage(x, seg, e, aw, dw, vp):
    rows, seq = seg.shape
    tokens, width = x.shape
    own_rows, ff = dw.shape[1:]
    heads, chunks = width // HD, ff // width
    pairs = heads // 2
    pieces = pairs + 2 + 4 * chunks
    sh = jax.ShapeDtypeStruct
    dma = pltpu.SemaphoreType.DMA
    v = pltpu.VMEM
    hbm = pl.BlockSpec(memory_space=pl.ANY)
    vmem = pl.BlockSpec(memory_space=pltpu.VMEM)
    tok = sh((tokens, width), bf16)
    wide = sh((chunks, tokens, width), bf16)
    long = sh((tokens, width), f32)
    block = (2, 2, 2, 2, own_rows, LANES)
    scratch = [
        v((pieces, 3) + block, bf16), v(block, bf16), v((pieces, 3, own_rows, LANES), bf16), v((own_rows, LANES), bf16),
        v((LANES, LANES), f32), v((tokens, width), bf16), v((tokens, width), bf16), v((tokens, width), bf16),
        v((tokens, width), f32), v((tokens, width), bf16), v((tokens, width), f32), v((chunks, tokens, width), f32),
        v((chunks, tokens, width), bf16), v((tokens, width), bf16), v((rows, seq, seq), f32), v((rows, seq, LANES), f32),
        v((chunks, 1, width), f32), v((tokens, LANES), f32),
        dma((6 + 2 * chunks,)), dma((pairs + 7 + 2 * chunks,)), dma((pieces,)), dma((3, tokens // 256)),
    ] + [dma((pieces,))] * 11 + [dma(())] * 9
    return pl.pallas_call(
        functools.partial(stage_kernel, heads),
        out_shape=(sh((pairs, tokens, PIECE), bf16), tok, sh((rows, 16, seq), f32), sh((pieces, 3) + block, bf16), tok, tok, wide,
                   sh((chunks, tokens, width), f32), tok, long, long, sh((tokens, LANES), f32), sh((8, width), f32), sh((16, width), f32)),
        in_specs=[hbm, vmem, hbm, hbm, hbm, vmem],
        out_specs=(hbm, hbm, vmem) + (hbm,) * 9 + (vmem, vmem),
        scratch_shapes=scratch,
        compiler_params=pltpu.CompilerParams(collective_id=0, has_side_effects=True, vmem_limit_bytes=BIG),
        name="stage",
    )(x, seg, e, aw, dw, vp)


class Reduce:
    def __init__(self, place, part, froms, done, out, sems, pieces, tiles=3):
        self.p, self.part, self.done, self.out, self.pieces, self.whole = place, part, done, out, pieces, tiles == 1
        self.names = ("core", "y", "p") if self.whole else ("core", "y", "p", "x", "early_y", "late_x")
        self.froms = dict(zip(("core", "y", "p", "z", "x", "early_y"), froms))
        self.zs, self.zr = sems[:2]
        self.sems = {name: (sems[2 + 2 * k], sems[3 + 2 * k]) for k, name in enumerate(self.names)}
        self.own = pl.ds(0, 1) if self.whole else pl.ds(place.x, 2)
        self.most = slice(None) if self.whole else pl.ds(0, 3)

    def copy(self, name, i):
        p, f, landing = self.p, self.part, self.froms
        if name == "core":
            src, dst = f.at[i, :, :, :, 1 - p.core], landing[name].at[i]
        elif name == "x":
            src, dst = f.at[i, 2 * (1 - p.x), self.most, :, p.core], landing[name].at[i, self.most]
        elif name == "late_x":
            src, dst = f.at[i, 2 * (1 - p.x), 3, p.y, p.core], landing["x"].at[i, 3, 0]
        elif name == "y":
            src, dst = f.at[i, self.own, self.most, 1 - p.y, p.core], landing[name].at[i, :, self.most]
        elif name == "early_y":
            src, dst = f.at[i, :, 3, 1 - p.y, p.core], landing[name].at[i]
        else:
            src, dst = self.done.at[i], landing[name].at[i]
        send, recv = self.sems[name]
        axis = {"p": "x", "early_y": "y", "late_x": "x"}.get(name, name)
        return remote(src, dst, send.at[i], recv.at[i], p.over(axis))

    def z_copy(self, i, k, incoming=False):
        p = self.p
        peer = p.z_peer(k)
        came = peer if incoming else p.z
        return remote(self.part.at[i, self.own, peer, p.y, p.core], self.froms["z"].at[i, came], self.zs.at[i, k], self.zr.at[i, came], p.over(k))

    def start(self, i):
        self.copy("core", i).start()

    def add(self, at, term):
        self.part[at] = self.part[at] + term

    def x_step(self, i):
        p = self.p
        self.copy("core", i).wait_recv()
        for t in range(1 if self.whole else 3):
            self.add((i, t, slice(None), slice(None), p.core), self.froms["core"][i, t])
        for name in ("y",) if self.whole else ("x", "early_y"):
            self.copy(name, i).start()

    def y_step(self, i):
        p = self.p
        self.copy("early_y", i).wait_recv()
        self.add((i, slice(None), 3, p.y, p.core), self.froms["early_y"][i])
        self.copy("late_x", i).start()
        self.copy("x", i).wait_recv()
        self.add((i, 2 * p.x, self.most, slice(None), p.core), self.froms["x"][i, :3])
        self.copy("y", i).start()

    def z_step(self, i):
        p = self.p
        self.copy("y", i).wait_recv()
        self.add((i, self.own, self.most, p.y, p.core), self.froms["y"][i, :, self.most])
        if not self.whole:
            self.copy("late_x", i).wait_recv()
            self.add((i, 2 * p.x, 3, p.y, p.core), self.froms["x"][i, 3, 0])
        for k in (2, 1, 3):
            self.z_copy(i, k).start()

    def p_step(self, i):
        p, f = self.p, self.part
        total = f[i, self.own, p.z, p.y, p.core].astype(f32)
        for k in (1, 2, 3):
            self.z_copy(i, k, True).wait_recv()
            total += self.froms["z"][i, p.z_peer(k)].astype(f32)
        self.done[i] = total.astype(bf16)
        self.copy("p", i).start()

    def finish(self, i):
        self.copy("p", i).wait_recv()
        a, b = self.done[i].astype(f32), self.froms["p"][i].astype(f32)
        if self.whole:
            self.out[i] = a[0] + b[0]
            return
        first = self.p.x == 0
        low, high = jnp.where(first, a, b), jnp.where(first, b, a)
        self.out[i] = jnp.concatenate([low[0], low[1] + high[0], high[1]], 1)

    def later(self, t):
        for lag, step in zip(REDUCE_LAGS, (self.y_step, self.z_step, self.p_step, self.finish)):
            when((t >= lag) & (t < self.pieces + lag), lambda lag=lag, step=step: step(t - lag))

    def turn(self, t):
        when(t < self.pieces, lambda: self.x_step(t))
        self.later(t)

    def sent(self, i):
        for name in self.names:
            self.copy(name, i).wait_send()
        for k in (1, 2, 3):
            self.z_copy(i, k).wait_send()


def back_kernel(heads, x_hbm, c_hbm, y1_hbm, dz_hbm, dh2_hbm, n1_hbm, r1_hbm, g_hbm, gp_hbm, qkv_hbm, w_hbm,
                seg_ref, lse_ref, dv_ref, vec_ref, gin_o, sum_o, vsum_o,
                part, fromc, fromy, fromp, fromz, fromx, frome, done, vpart, vfromc, vfromy, vfromp, vfromz, vdone, pool, wpool, gpool, acc, cb, dab, dcb, r1b, delta, vrow,
                ld, out_sem, *sems):
    place = Place()
    rows, seq = seg_ref.shape
    tokens, width = x_hbm.shape
    pairs = heads // 2
    chunks = g_hbm.shape[0]
    own_rows = part.shape[-2]
    pieces = part.shape[0]
    big = 512
    r_ = Reduce(place, part, (fromc, fromy, fromp, fromz, fromx, frome), done, sum_o, sems[:14], pieces)
    rv = Reduce(place, vpart, (vfromc, vfromy, vfromp, vfromz), vdone, vsum_o, sems[14:], vpart.shape[0], 1)
    ff_pieces = 4 * chunks
    first_ff = pairs + 2
    du, dz, y1 = pool.at[2], pool.at[3], pool.at[4]
    x = y1

    def load(k, src, dst):
        return pltpu.make_async_copy(src, dst, ld.at[k])

    g_in = [load(j, g_hbm.at[j], pool.at[j % 2]) for j in range(chunks)]
    gp_in = [load(chunks + j, gp_hbm.at[j], gpool.at[j % 2]) for j in range(chunks)]
    w_in = [load(2 * chunks + j, w_hbm.at[pl.ds(first_ff + 4 * j, 4)], wpool.at[pl.ds(4 * (j % 2), 4)]) for j in range(chunks)]
    base = 3 * chunks
    dz_in, y1_in, acc_in, c_in, r1_in = (load(base + k, s, d) for k, (s, d) in enumerate(
        ((dz_hbm, dz), (y1_hbm, y1), (dh2_hbm, acc), (c_hbm, cb), (r1_hbm, r1b))))
    base += 5
    n1_in = load(base, n1_hbm, gpool.at[0])
    wo_in = load(base + 1, w_hbm.at[pl.ds(pairs, 2)], wpool.at[pl.ds(0, 2)])
    wq_in = load(base + 2, w_hbm.at[pl.ds(0, pairs)], wpool.at[pl.ds(2, pairs)])
    x_in = load(base + 3, x_hbm, x)
    base += 4

    def q_in(p):
        return load(base + p, qkv_hbm.at[p], pool.at[3, :, pl.ds(pl.multiple_of(lax.rem(p, 2) * PIECE, LANES), PIECE)])

    for c in (dz_in, g_in[0]):
        c.start()
    place.greet(place.reduce_peers)
    place.met(place.reduce_peers)
    vrow[...] = jnp.zeros_like(vrow)
    vrow[:8, :] = dv_ref[...]

    def colsum(t):
        return jnp.sum(t, 0, keepdims=True)

    half = width // 2

    def weight_grad(left, right, piece, count):
        d = dot_tn(left[...], right)
        for t in range(3 * count):
            part[piece + t // 3, t % 3] = d[:, t * LANES : (t + 1) * LANES].astype(bf16).reshape(4, 2, 2, own_rows, LANES)
        for k in range(count):
            r_.start(piece + k)

    dz_in.wait()
    for j in range(chunks):
        s = j % 2
        g_in[j].wait()
        if j == 0:
            for c in (gp_in[0], w_in[0], acc_in, y1_in, g_in[1], gp_in[1], w_in[1], c_in, r1_in):
                c.start()
        weight_grad(dz, pool[s], 4 * j, 2)
        r_.turn(3 * j)
        gp_in[j].wait()
        w_in[j].wait()
        if j == 0:
            y1_in.wait()
            acc_in.wait()

        def block(i, j=j, s=s):
            at = pl.ds(pl.multiple_of(i * big, big), big)
            d = (dot(dz[at, :], columns(wpool, 4 * s + 2, 4 * s + 3)) * gpool[s, at, :]).astype(bf16)
            du[at, :] = d
            acc[at, :] += dot_nt(d, columns(wpool, 4 * s, 4 * s + 1))
            vrow[8 + j : 9 + j, :] += colsum(d.astype(f32))

        loop(tokens // big, block)
        r_.turn(3 * j + 1)
        if j + 2 < chunks:
            g_in[j + 2].start()
            gp_in[j + 2].start()
            w_in[j + 2].start()
        if j == chunks - 2:
            n1_in.start()
            wo_in.start()
        weight_grad(y1, du[...], 4 * j + 2, 2)
        r_.turn(3 * j + 2)
    wq_in.start()
    x_in.start()
    q_in(0).start()
    q_in(1).start()
    for r in range(rows):
        segf = seg_ref[r : r + 1, :].astype(f32)
        rep = jnp.broadcast_to(segf, (LANES, seq)).T
        for k in range(seq // LANES):
            sl = slice(k * LANES, (k + 1) * LANES)
            gpool[1, r * seq : (r + 1) * seq, sl] = jnp.where(rep == segf[:, sl], 0.0, NEG)
    c_in.wait()
    r1_in.wait()
    n1_in.wait()
    wo_in.wait()
    g1 = vec_ref[0:1, :]
    sel_shape = (delta.shape[0], width)
    sel = jnp.where(lax.broadcasted_iota(jnp.int32, sel_shape, 0) == lax.broadcasted_iota(jnp.int32, sel_shape, 1) // HD, 1.0, 0.0).astype(bf16)

    def norm_one_back(i):
        at = pl.ds(pl.multiple_of(i * 256, 256), 256)
        dy1 = acc[at, :]
        n1 = gpool[0, at, :]
        dn = dy1 * g1
        r1 = r1b[at, :1]
        dh1 = r1 * (dn - jnp.mean(dn, 1, keepdims=True) - n1 * jnp.mean(dn * n1, 1, keepdims=True))
        acc[at, :] = dh1
        da = dh1.astype(bf16)
        dab[at, :] = da
        dc = dot_nt(da, columns(wpool, 0, 1)).astype(bf16)
        dcb[at, :] = dc
        prod = dc.astype(f32) * cb[at, :].astype(f32)
        hi = prod.astype(bf16)
        lo = (prod - hi.astype(f32)).astype(bf16)
        delta[:, at] = dot_nt(sel, hi) + dot_nt(sel, lo)
        vrow[0:1, :] += colsum(dy1 * n1)
        vrow[1:2, :] += colsum(dy1)
        vrow[6:7, :] += colsum(da.astype(f32))

    loop(tokens // 256, norm_one_back)
    r_.turn(3 * chunks)
    weight_grad(cb, dab[...], ff_pieces, 2)
    r_.turn(3 * chunks + 1)
    t0 = 3 * chunks + 2
    twice = ff_pieces + 2 - t0
    x_in.wait()
    first_seq = lax.broadcasted_iota(jnp.int32, (seq, LANES), 1) < HD

    def pair(p, last=False):
        head = pl.ds(pl.multiple_of(p * LANES, LANES), LANES)
        col = pl.multiple_of(lax.rem(p, 2) * PIECE, LANES)
        to = p // 2
        q_in(p).wait()

        def row(r):
            tok = pl.ds(pl.multiple_of(r * seq, seq), seq)
            q2 = pool[3, tok, pl.ds(col, LANES)]
            k2 = pool[3, tok, pl.ds(col + LANES, LANES)]
            v2 = pool[3, tok, pl.ds(col + 2 * LANES, LANES)]
            dc2 = dcb[tok, head]
            zero = jnp.zeros_like(k2)
            near = gpool[1, tok, :seq]
            grads = []
            for h in range(2):
                lse = lse_ref[r, pl.ds(2 * p + h, 1), :]
                dl = delta[pl.ds(2 * p + h, 1), tok]
                own = first_seq if h == 0 else ~first_seq
                pt = jnp.exp2((dot_nt(jnp.where(own, k2, zero), q2) + near) * SCALE2 - lse)
                ds = (pt * (dot_nt(jnp.where(own, v2, zero), dc2) - dl)).astype(bf16)
                dv = dot(pt.astype(bf16), dc2)
                grads.append((dot_tn(ds, k2) * 0.125, dot(ds, q2) * 0.125, dv))
            for k, (a, b) in enumerate(zip(*grads)):
                pool[to, tok, pl.ds(col + k * LANES, LANES)] = jnp.where(first_seq, a, b).astype(bf16)
            if last:
                r_.later(t0 + p + twice + 1 + r)
            else:
                when((r == 0) & (p < twice), lambda: r_.turn(t0 + 2 * p))
                when((r == 0) & (p == twice), lambda: r_.later(t0 + 2 * p))

        loop(rows, row)
        if not last:
            when(p + 2 < pairs, lambda: q_in(p + 2).start())
        d = pool[to, :, pl.ds(col, PIECE)]

        def biases():
            sums = colsum(d.astype(f32))
            vrow[4:5, head] = sums[:, :LANES]
            vrow[5:6, head] = sums[:, 2 * LANES :]

        if last:
            def product(a):
                w = dot_tn(x[:, pl.ds(pl.multiple_of(a * half, LANES), half)], d)
                for t in range(3):
                    vpart[t, 0, pl.ds(2 * a, 2)] = w[:, t * LANES : (t + 1) * LANES].astype(bf16).reshape(2, 2, 2, own_rows, LANES)

            loop(2, product)
            for t in range(3):
                rv.start(t)
            biases()
            vpart[3, 0] = vrow[...].T.astype(bf16).reshape(4, 2, 2, own_rows, LANES)
            rv.start(3)
        else:
            weight_grad(x, d, ff_pieces + 2 + p, 1)
            biases()
            late = p >= twice
            done = t0 + p + jnp.minimum(p + 1, twice)
            r_.x_step(done)
            r_.later(jnp.where(late, done + 1, done))

    loop(pairs - 1, pair)
    pair(pairs - 1, True)
    t0 += pairs + twice + rows
    singles = vpart.shape[0]
    wq_in.wait()
    blocks = tokens // 256

    def gin_block(i):
        at = pl.ds(pl.multiple_of(i * 256, 256), 256)
        d = jnp.concatenate([pool[k, at, :] for k in range(pairs // 2)], 1)
        dcb[at, :] = (acc[at, :] + dot_nt(d, columns(wpool, *range(2, 2 + pairs)))).astype(bf16)
        when(i == 0, lambda: loop(singles, rv.x_step))
        when(i < 2, lambda: r_.turn(t0 + i))
        when(i == 2, lambda: loop(singles, rv.z_step))
        when(i == 3, lambda: r_.turn(t0 + 2))

    loop(blocks, gin_block)
    gin_out = pltpu.make_async_copy(dcb, gin_o, out_sem)
    gin_out.start()
    t0 += 3
    rest = pieces + REDUCE_LAGS[-1] - t0

    def rest_turn(i):
        r_.turn(t0 + i)
        when(i == 0, lambda: loop(singles, rv.p_step))

    loop(rest, rest_turn)
    loop(singles, rv.finish)
    loop(pieces, r_.sent)
    loop(singles, rv.sent)
    gin_out.wait()


def back(x, c, y1, dz, dh2, n1, r1, g, gp, qkv, w, seg, lse, dv, vec):
    rows, seq = seg.shape
    tokens, width = x.shape
    chunks = g.shape[0]
    own_rows = w.shape[-2]
    heads = width // HD
    pairs = heads // 2
    pieces = 4 * chunks + 2 + pairs - 1
    sh = jax.ShapeDtypeStruct
    dma = pltpu.SemaphoreType.DMA
    v = pltpu.VMEM
    hbm = pl.BlockSpec(memory_space=pl.ANY)
    vmem = pl.BlockSpec(memory_space=pltpu.VMEM)
    tail = (own_rows, LANES)
    tok = v((tokens, width), bf16)
    scratch = [
        v((pieces, 3, 4, 2, 2) + tail, bf16), v((pieces, 3, 4, 2) + tail, bf16), v((pieces, 2, 4) + tail, bf16), v((pieces, 2) + tail, bf16),
        v((pieces, 4, 2) + tail, bf16), v((pieces, 4, 2) + tail, bf16), v((pieces, 3) + tail, bf16), v((pieces, 2) + tail, bf16),
        v((4, 1, 4, 2, 2) + tail, bf16), v((4, 1, 4, 2) + tail, bf16), v((4, 1, 4) + tail, bf16), v((4, 1) + tail, bf16),
        v((4, 4, 1) + tail, bf16), v((4, 1) + tail, bf16), v((5, tokens, width), bf16), v((8,) + w.shape[1:], bf16), v((2, tokens, width), f32),
        v((tokens, width), f32), tok, tok, tok, v((tokens, LANES), f32), v((16, tokens), f32),
        v((LANES, width), f32),
        dma((3 * chunks + 9 + pairs,)), dma(())] + [dma((pieces, 4))] * 2 + [dma((pieces,))] * 12 + [dma((4, 4))] * 2 + [dma((4,))] * 6
    return pl.pallas_call(
        functools.partial(back_kernel, heads),
        out_shape=(sh((tokens, width), bf16), sh((pieces, own_rows, PIECE), f32), sh((4, own_rows, LANES), f32)),
        in_specs=[hbm] * 11 + [vmem] * 4,
        out_specs=(hbm, vmem, vmem),
        scratch_shapes=scratch,
        compiler_params=pltpu.CompilerParams(collective_id=1, has_side_effects=True, vmem_limit_bytes=63 * 2**20),
        name="back",
    )(x, c, y1, dz, dh2, n1, r1, g, gp, qkv, w, seg, lse, dv, vec)


def update_kernel(rates, sum_ref, vsum_ref, gin_hbm, out_hbm, am, aw, aa, dm, dw, da, vm, vw, va,
                  gin_o, out_o, am_o, aw_o, aa_o, dm_o, dw_o, da_o, vm_o, vw_o, va_o, square, tok, att, den, ld, st):
    matrix, vector, replicas = rates
    moves = [(dm, den.at[0], dm_o), (dw, den.at[1], dw_o), (da, den.at[2], da_o), (am, att.at[0], am_o), (aw, att.at[1], aw_o),
             (aa, att.at[2], aa_o), (gin_hbm, tok.at[0], gin_o), (out_hbm, tok.at[1], out_o)]
    loads = [pltpu.make_async_copy(s, d, ld.at[k]) for k, (s, d, _) in enumerate(moves)]
    stores = [pltpu.make_async_copy(d, o, st.at[k]) for k, (_, d, o) in enumerate(moves)]
    for c in loads:
        c.start()

    def advance(grad, rate, moment, weight, average):
        grad = grad / replicas
        moment = momentum_decay * moment + grad
        weight = weight - rate * (grad + momentum_decay * moment)
        return moment, weight, average_decay * average + (1.0 - average_decay) * weight

    def advance_in(grad, ref, index):
        news = advance(grad, matrix, *(ref[(k,) + index] for k in range(3)))
        for k in range(3):
            ref[(k,) + index] = news[k]

    rows, own = vm.shape
    square[...] = jnp.zeros_like(square)
    square[:own, :] = vsum_ref[3]
    vm_o[...], vw_o[...], va_o[...] = advance(square[...].T[:rows, :own], vector, vm[...], vw[...], va[...])
    every = slice(None)
    pairs = att.shape[3] // LANES
    ff_pieces = sum_ref.shape[0] - 1 - pairs
    for c in loads[:3]:
        c.wait()
    for i in range(ff_pieces):
        col = i // 4 * 2 * PIECE + i % 2 * PIECE
        advance_in(sum_ref[i], den, (1 - i % 4 // 2, every, slice(col, col + PIECE)))
    for c in stores[:3]:
        c.start()
    for c in loads[3:6]:
        c.wait()
    for i in range(2):
        advance_in(sum_ref[ff_pieces + i], att, (3, every, slice(i * PIECE, (i + 1) * PIECE)))
    for p in range(pairs):
        for k in range(3):
            grad = vsum_ref[k] if p == pairs - 1 else sum_ref[ff_pieces + 2 + p, :, k * LANES : (k + 1) * LANES]
            advance_in(grad, att, (k, every, slice(p * LANES, (p + 1) * LANES)))
    for c in loads[6:]:
        c.wait()
    for c in stores[3:]:
        c.start()
    for c in stores:
        c.wait()


def update(rates, sums, vsums, gin, out, states):
    am, dm = states[0], states[3]
    sh = jax.ShapeDtypeStruct
    v = pltpu.VMEM
    hbm = pl.BlockSpec(memory_space=pl.ANY)
    vmem = pl.BlockSpec(memory_space=pltpu.VMEM)
    places = [hbm] * 8 + [vmem] * 3
    return pl.pallas_call(
        functools.partial(update_kernel, rates),
        out_shape=(sh(gin.shape, bf16), sh(out.shape, bf16)) + tuple(sh(s.shape, f32) for s in states),
        in_specs=[vmem, vmem] + places,
        out_specs=tuple(places),
        scratch_shapes=[v((LANES, LANES), f32), v((2,) + gin.shape, bf16), v((3,) + am.shape, f32), v((3,) + dm.shape, f32),
                        pltpu.SemaphoreType.DMA((8,)), pltpu.SemaphoreType.DMA((8,))],
        compiler_params=pltpu.CompilerParams(vmem_limit_bytes=BIG),
        name="update",
    )(sums, vsums, gin, out, *states)


def pack_columns(attention, dense, vectors):
    count = vectors.shape[0]
    vector_cols = jnp.pad(vectors.T, ((0, 0), (0, 128 - count)))
    first = jnp.concatenate([attention[0], attention[1], attention[2], vector_cols], 1)
    second = jnp.concatenate([attention[3], dense[0], dense[1]], 1)
    return first, second


def advance(gradient, moment, weight, average, step_rate):
    moment_new = momentum_decay * moment + gradient
    weight_new = weight - step_rate * (gradient + momentum_decay * moment_new)
    average_new = average_decay * average + (1.0 - average_decay) * weight_new
    return (moment_new, weight_new, average_new)


def plain_body(
    hidden_in,
    segment_ids,
    cotangent,
    attention_weights,
    attention_momentum,
    attention_average,
    dense_weights,
    dense_momentum,
    dense_average,
    vector_params,
    vector_momentum,
    vector_average,
):
    row_count, length, width = hidden_in.shape
    ff = dense_weights.shape[-1]
    vector_rows = vector_params.shape[0]
    x = hidden_in.reshape(-1, width)
    e = cotangent.reshape(-1, width)
    first, second = pack_columns(attention_weights, dense_weights, vector_params)
    first_full = lax.all_gather(first.astype(bf16), "wide", axis=0, tiled=True)
    second_full = lax.all_gather(second.astype(bf16), "wide", axis=0, tiled=True)
    vec = first_full[:, 3 * width : 3 * width + vector_rows].astype(f32).T
    bias_qkv = jnp.concatenate([vec[4:5], jnp.zeros((1, width), f32), vec[5:6]], 1)
    w_qkv = first_full[:, : 3 * width]
    wo, win, wd = (second_full[:, :width], second_full[:, width : width + ff], second_full[:, width + ff :])
    qkv, c, lse = attn_fwd(x, segment_ids, w_qkv, bias_qkv)
    out, y1, g, dz, du, da, dc, dh1, delta, dvec, dbin = mid(
        x, c, e, wo, win, wd, vec, vec[8:].reshape(1, ff)
    )
    grad_second = jnp.concatenate([wgrad(c, da), wgrad(y1, du), wgrad(dz, g)], 1)
    share_second = lax.psum_scatter(grad_second, "wide", scatter_dimension=0, tiled=True)
    dqkv, gin, dw, db = attn_bwd(segment_ids, qkv, dc, lse, delta, dh1, w_qkv, x)
    dvec = jnp.concatenate(
        [dvec[:4], db[:, :width], db[:, 2 * width :], dvec[6:8], dbin.reshape(-1, width)], 0
    )
    grad_first = jnp.concatenate(
        [dw, jnp.pad(dvec.T, ((0, 0), (0, 128 - vector_rows))).astype(bf16)], 1
    )
    share_first = lax.psum_scatter(grad_first, "wide", scatter_dimension=0, tiled=True)
    replicas = lax.axis_size("narrow")
    tokens_all = row_count * length * lax.axis_size("wide") * replicas
    grad_scale = math.sqrt(tokens_all) / replicas
    t1 = lax.psum(share_first, "narrow").astype(f32) / replicas
    t2 = lax.psum(share_second, "narrow").astype(f32) / replicas
    cut = lambda t, j: t[:, j * width : (j + 1) * width]
    attention_grad = jnp.stack([cut(t1, 0), cut(t1, 1), cut(t1, 2), cut(t2, 0)])
    dense_grad = jnp.stack([t2[:, width : width + ff], t2[:, width + ff :]])
    vector_grad = t1[:, 3 * width : 3 * width + vector_rows].T
    attention_new = advance(attention_grad, attention_momentum, attention_weights, attention_average, matrix_rate / grad_scale)
    dense_new = advance(dense_grad, dense_momentum, dense_weights, dense_average, matrix_rate / grad_scale)
    vector_new = advance(vector_grad, vector_momentum, vector_params, vector_average, vector_rate / grad_scale)
    return (out.reshape(hidden_in.shape), gin.reshape(hidden_in.shape)) + attention_new + dense_new + vector_new


def body(
    hidden_in,
    segment_ids,
    cotangent,
    attention_weights,
    attention_momentum,
    attention_average,
    dense_weights,
    dense_momentum,
    dense_average,
    vector_params,
    vector_momentum,
    vector_average,
):
    row_count, length, width = hidden_in.shape
    x = hidden_in.reshape(-1, width)
    e = cotangent.reshape(-1, width)
    replicas = lax.axis_size("narrow")
    tokens_all = row_count * length * lax.axis_size("wide") * replicas
    grad_scale = math.sqrt(tokens_all) / replicas
    rates = (matrix_rate / grad_scale, vector_rate / grad_scale, replicas)
    qkv, c, lse, w, out, y1, g, gp, dz, dh2, n1, r1, dv, vec = stage(
        x, segment_ids, e, attention_weights, dense_weights, vector_params
    )
    states = (
        attention_momentum, attention_weights, attention_average,
        dense_momentum, dense_weights, dense_average,
        vector_momentum, vector_params, vector_average,
    )
    gin, sums, vsums = back(x, c, y1, dz, dh2, n1, r1, g, gp, qkv, w, segment_ids, lse, dv, vec)
    news = update(rates, sums, vsums, gin, out, states)
    return (news[1].reshape(hidden_in.shape), news[0].reshape(hidden_in.shape)) + tuple(news[2:])


def solution(mesh):
    token = P(("wide", "narrow"), None, None)
    matrix = P(None, "wide", None)
    vector = P(None, "wide")
    in_specs = (token, P(("wide", "narrow"), None), token) + (matrix,) * 6 + (vector,) * 3
    out_specs = (token, token) + (matrix,) * 6 + (vector,) * 3
    ours = mesh.shape["wide"] == 16 and mesh.shape["narrow"] == 2
    return jax.shard_map(body if ours else plain_body, mesh=mesh, in_specs=in_specs, out_specs=out_specs, check_vma=False)
```

profile of v0, /device:TPU:0, one launch (start us, length us, event | category | flops | bytes accessed | tf_op | source)
XLA Modules:
  0.0 194.3 jit_solution(14682742449098746448)
XLA Ops:
  0.6 88.1 %stage.1 = (bf16[6,1024,384]{2,1,0:T(8,128)(2,1)}, bf16[1024,768]{1,0:T(8,128)(2,1)}, f32[2,16,512]{2,1,0:T(8,128)}, bf16[24,3,2,2,2,2,48,128]{7,6,5,4,3,2,1,0:T...) custom-call(bf16[1024,768]{1,0:T(8,128)(2,1)} %bitcast.4, ...), custom_call_target="tpu_custom_call" | custom-call | tf_op jit(solution)/shard_map/stage/pallas_call | solution.py:709
  88.8 97.1 %back.1 = (bf16[1024,768]{1,0:T(8,128)(2,1)}, f32[23,48,384]{2,1,0:T(8,128)}, f32[4,48,128]{2,1,0:T(8,128)}) custom-call(bf16[1024,768]{1,0:T(8,128)(2,1)} %bitcast.5, bf16[1024,768]{1,0:T(8,128)(2,1)} %get-tuple-element.39.c_hbm, bf16[1024,768]{1,0:T(8,128)(2,1)} %get-tuple-element.40.y1_hbm, bf16[1024,768]{1,0:T(8,128)(2,1)} %get-tuple-element.41.dz_hbm, ...), custom_call_target="tpu_custom_call" | custom-call | tf_op jit(solution)/shard_map/back/pallas_call | solution.py:1076
  185.9 8.2 %update.1 = (bf16[1024,768]{1,0:T(8,128)(2,1)}, bf16[1024,768]{1,0:T(8,128)(2,1)}, f32[4,48,768]{2,1,0:T(8,128)}, f32[4,48,768]{2,1,0:T(8,128)}, f32[4,48,768]{2...) custom-call(f32[23,48,384]{2,1,0:T(8,128)} %get-tuple-element.52.sum, ...), custom_call_target="tpu_custom_call" | custom-call | tf_op jit(solution)/shard_map/update/pallas_call | solution.py:1145
where the time goes:
time: 195 us; the launch traced here: 194 us
  Pallas kernels  193 us (99%)
    pallas_call x1, Pallas kernels, back(): pl.pallas_call(functools.partial(back_kernel, heads), out_shape=(sh((toke...  97.1 us
    pallas_call x1, Pallas kernels, stage(): pl.pallas_call(functools.partial(stage_kernel, heads), out_shape=(sh((pai...  88.1 us
    pallas_call x1, Pallas kernels, update(): pl.pallas_call(functools.partial(update_kernel, rates), out_shape=(sh(gin...  8.19 us

commit v1 on v0

--- a/solution.py
+++ b/solution.py
@@ -830,7 +830,6 @@
     chunks = g_hbm.shape[0]
     own_rows = part.shape[-2]
     pieces = part.shape[0]
-    big = 512
     r_ = Reduce(place, part, (fromc, fromy, fromp, fromz, fromx, frome), done, sum_o, sems[:14], pieces)
     rv = Reduce(place, vpart, (vfromc, vfromy, vfromp, vfromz), vdone, vsum_o, sems[14:], vpart.shape[0], 1)
     ff_pieces = 4 * chunks
@@ -841,9 +840,15 @@
     def load(k, src, dst):
         return pltpu.make_async_copy(src, dst, ld.at[k])
 
-    g_in = [load(j, g_hbm.at[j], pool.at[j % 2]) for j in range(chunks)]
-    gp_in = [load(chunks + j, gp_hbm.at[j], gpool.at[j % 2]) for j in range(chunks)]
-    w_in = [load(2 * chunks + j, w_hbm.at[pl.ds(first_ff + 4 * j, 4)], wpool.at[pl.ds(4 * (j % 2), 4)]) for j in range(chunks)]
+    def g_in(j):
+        return load(j, g_hbm.at[j], pool.at[lax.rem(j, 2)])
+
+    def gp_in(j):
+        return load(chunks + j, gp_hbm.at[j], gpool.at[lax.rem(j, 2)])
+
+    def w_in(j):
+        return load(2 * chunks + j, w_hbm.at[pl.ds(first_ff + 4 * j, 4)], wpool.at[pl.ds(4 * lax.rem(j, 2), 4)])
+
     base = 3 * chunks
     dz_in, y1_in, acc_in, c_in, r1_in = (load(base + k, s, d) for k, (s, d) in enumerate(
         ((dz_hbm, dz), (y1_hbm, y1), (dh2_hbm, acc), (c_hbm, cb), (r1_hbm, r1b))))
@@ -857,7 +862,7 @@
     def q_in(p):
         return load(base + p, qkv_hbm.at[p], pool.at[3, :, pl.ds(pl.multiple_of(lax.rem(p, 2) * PIECE, LANES), PIECE)])
 
-    for c in (dz_in, g_in[0]):
+    for c in (dz_in, g_in(0)):
         c.start()
     place.greet(place.reduce_peers)
     place.met(place.reduce_peers)
@@ -877,38 +882,52 @@
             r_.start(piece + k)
 
     dz_in.wait()
-    for j in range(chunks):
-        s = j % 2
-        g_in[j].wait()
-        if j == 0:
-            for c in (gp_in[0], w_in[0], acc_in, y1_in, g_in[1], gp_in[1], w_in[1], c_in, r1_in):
+
+    def chunk(j):
+        s = lax.rem(j, 2)
+        g_in(j).wait()
+
+        def rest_of_loads():
+            for c in (gp_in(0), w_in(0), acc_in, y1_in, g_in(1), gp_in(1), w_in(1), c_in, r1_in):
                 c.start()
+
+        when(j == 0, rest_of_loads)
         weight_grad(dz, pool[s], 4 * j, 2)
         r_.turn(3 * j)
-        gp_in[j].wait()
-        w_in[j].wait()
-        if j == 0:
+        gp_in(j).wait()
+        w_in(j).wait()
+
+        def first_waits():
             y1_in.wait()
             acc_in.wait()
 
-        def block(i, j=j, s=s):
-            at = pl.ds(pl.multiple_of(i * big, big), big)
+        when(j == 0, first_waits)
+
+        def block(i):
+            at = pl.ds(pl.multiple_of(i * 512, 512), 512)
             d = (dot(dz[at, :], columns(wpool, 4 * s + 2, 4 * s + 3)) * gpool[s, at, :]).astype(bf16)
             du[at, :] = d
             acc[at, :] += dot_nt(d, columns(wpool, 4 * s, 4 * s + 1))
-            vrow[8 + j : 9 + j, :] += colsum(d.astype(f32))
-
-        loop(tokens // big, block)
+            vrow[pl.ds(8 + j, 1), :] += colsum(d.astype(f32))
+
+        loop(tokens // 512, block)
         r_.turn(3 * j + 1)
-        if j + 2 < chunks:
-            g_in[j + 2].start()
-            gp_in[j + 2].start()
-            w_in[j + 2].start()
-        if j == chunks - 2:
+
+        def ahead():
+            for c in (g_in(j + 2), gp_in(j + 2), w_in(j + 2)):
+                c.start()
+
+        when(j + 2 < chunks, ahead)
+
+        def norm_loads():
             n1_in.start()
             wo_in.start()
+
+        when(j == chunks - 2, norm_loads)
         weight_grad(y1, du[...], 4 * j + 2, 2)
         r_.turn(3 * j + 2)
+
+    loop(chunks, chunk)
     wq_in.start()
     x_in.start()
     q_in(0).start()

time: 195 us -> 194 us (level)
  no operation moved by 1% of the time
where the time goes in v1:
time: 194 us
  Pallas kernels  193 us (99%)
    pallas_call x1, Pallas kernels, back(): pl.pallas_call(functools.partial(back_kernel, heads), out_shape=(sh((toke...  96.5 us
    pallas_call x1, Pallas kernels, stage(): pl.pallas_call(functools.partial(stage_kernel, heads), out_shape=(sh((pai...  88.1 us
    pallas_call x1, Pallas kernels, update(): pl.pallas_call(functools.partial(update_kernel, rates), out_shape=(sh(gin...  8.19 us

profile of v1, /device:TPU:0, one launch (start us, length us, event | category | flops | bytes accessed | tf_op | source)
XLA Modules:
  0.0 193.7 jit_solution(7656039674605405282)
XLA Ops:
  0.6 88.1 %stage.1 = (bf16[6,1024,384]{2,1,0:T(8,128)(2,1)}, bf16[1024,768]{1,0:T(8,128)(2,1)}, f32[2,16,512]{2,1,0:T(8,128)}, bf16[24,3,2,2,2,2,48,128]{7,6,5,4,3,2,1,0:T...) custom-call(bf16[1024,768]{1,0:T(8,128)(2,1)} %bitcast.4, ...), custom_call_target="tpu_custom_call" | custom-call | tf_op jit(solution)/shard_map/stage/pallas_call | solution.py:709
  88.8 96.5 %back.1 = (bf16[1024,768]{1,0:T(8,128)(2,1)}, f32[23,48,384]{2,1,0:T(8,128)}, f32[4,48,128]{2,1,0:T(8,128)}) custom-call(bf16[1024,768]{1,0:T(8,128)(2,1)} %bitcast.5, bf16[1024,768]{1,0:T(8,128)(2,1)} %get-tuple-element.39.c_hbm, bf16[1024,768]{1,0:T(8,128)(2,1)} %get-tuple-element.40.y1_hbm, bf16[1024,768]{1,0:T(8,128)(2,1)} %get-tuple-element.41.dz_hbm, ...), custom_call_target="tpu_custom_call" | custom-call | tf_op jit(solution)/shard_map/back/pallas_call | solution.py:1095
  185.3 8.2 %update.1 = (bf16[1024,768]{1,0:T(8,128)(2,1)}, bf16[1024,768]{1,0:T(8,128)(2,1)}, f32[4,48,768]{2,1,0:T(8,128)}, f32[4,48,768]{2,1,0:T(8,128)}, f32[4,48,768]{2...) custom-call(f32[23,48,384]{2,1,0:T(8,128)} %get-tuple-element.52.sum, ...), custom_call_target="tpu_custom_call" | custom-call | tf_op jit(solution)/shard_map/update/pallas_call | solution.py:1164
